TPU v7x, 256 devices: a whole 4x4x8 slice. The times are simulated.
256 devices in a mesh: owner: 16 (over z, core), tensor: 16 (over x, y).
Axes of the slice: x: 4, y: 4, z: 8, core: 2. Of those that a mesh axis runs over, the one named last changes fastest.
Arguments:
- mixer_input: bfloat16 [16384, 2, 8192], P('owner', None, 'tensor'), may hold values from -6 to 6
- step_raw: float32 [16384, 128], P('owner', 'tensor'), may hold values from -7 to 5
- decay_rate: float32 [128], P('tensor'), may hold values from 0.005 to 0.5
- skip_gain: float32 [128], P('tensor'), may hold values from 0.5 to 2
- state_proj: bfloat16 [16384, 2, 4, 256], P('owner'), may hold values from -1.5 to 1.5
- queries: bfloat16 [16384, 4096], P('owner', 'tensor'), may hold values from -256 to 256
- suffix_kv: bfloat16 [16384, 2, 4, 128], P('owner'), may hold values from -6 to 6
- state_pool: bfloat16 [64, 128, 64, 256], P('owner', 'tensor'), may hold values from -1.5 to 1.5
- page_pool: bfloat16 [256, 128, 2, 4, 128], P('owner'), may hold values from -6 to 6
- norm_gain: float32 [8192], P('tensor'), may hold values from 0.1 to 1.9
- hit_owner: int32 [64, 1], replicated, may hold values from 0 to 15; in each aligned block of 4 rows (0 to 3, 4 to 7, ...) at most 2 rows name the same one
- hit_slot: int32 [64], replicated, may hold values from 0 to 3
- page_owner: int32 [64, 16, 1], replicated, may hold values from 0 to 15; in each aligned block of 64 rows (0 to 63, 64 to 127, ..., all dimensions but the last counted through in order) at most 6 rows name the same one
- page_slot: int32 [64, 16], replicated, may hold values from 0 to 15
- prefix_len: int32 [64], replicated, may hold values from 256 to 2048, as said below
- suffix_len: int32 [64], replicated, may hold values from 64 to 256, as said below
Outputs:
- mamba_out: bfloat16 [16384, 8192], P('owner', 'tensor')
- attn_out: bfloat16 [16384, 4096], P('owner', 'tensor')
Inputs may be any that keep to these rules, and one draw needn't show every extreme that they name: `hit_owner`: the 4 requests on one index of owner name one owner at most 2 times, and some index reaches it. `page_owner`: of the 64 list entries of the requests on one index of owner, at most 6 name one owner, and some index reaches it. `prefix_len`: a multiple of 256; request 0 has 2048. `suffix_len`: request 0 has 256.
All inputs are finite; a program needn't handle non-finite values.
Results may differ from a plain program's by a relative error of at most 0.0045.
Values may be sent and summed in bfloat16 or wider, within the bound.
A program may use at most 192 MiB of HBM per device.

v0:
```python
import math
import jax
import jax.numpy as jnp
from jax import lax
from jax.sharding import PartitionSpec as P

SSM_HEAD_TOTAL = 128
MHDIM = 64
STATE = 256
GROUPS = 4
QHEADS = 32
KVHEADS = 4
HD = 128
PAGE = 128
SPAN = 128
SUF = 256
CAP_S = 2
MAXP = 16
EPSILON = 1e-05
NEG_FILL = -1e30


def mixer_core(x_heads, z_heads, rate_raw, decay_groups, skip_groups, b_rows, c_rows, start_state):
    seq_len, group_count, head_count, head_width = x_heads.shape
    blocks = seq_len // SPAN
    step_rate = jax.nn.softplus(rate_raw)
    keep_log = -step_rate * decay_groups[None]
    x_block = x_heads.reshape(blocks, SPAN, group_count, head_count, head_width)
    rate_block = step_rate.reshape(blocks, SPAN, group_count, head_count)
    cum_block = jnp.cumsum(keep_log.reshape(blocks, SPAN, group_count, head_count), axis=1)
    b_block = b_rows.reshape(blocks, SPAN, group_count, -1)
    c_block = c_rows.reshape(blocks, SPAN, group_count, -1)
    intersection = jnp.einsum(
        "cign,cjgn->cgij", c_block, b_block, preferred_element_type=jnp.float32
    )
    cum_moved = jnp.transpose(cum_block, (0, 2, 3, 1))
    rate_moved = jnp.transpose(rate_block, (0, 2, 3, 1))
    lower = jnp.arange(SPAN)[:, None] >= jnp.arange(SPAN)[None, :]
    fade = jnp.exp(jnp.where(lower, cum_moved[..., :, None] - cum_moved[..., None, :], NEG_FILL))
    weights = (intersection[:, :, None] * fade * rate_moved[..., None, :]).astype(jnp.bfloat16)
    inner = jnp.einsum("cghij,cjghp->cighp", weights, x_block, preferred_element_type=jnp.float32)
    cum_end = cum_block[:, -1]
    tail = jnp.exp(cum_end[:, None] - cum_block) * rate_block
    scaled = (tail[..., None] * x_block).astype(jnp.bfloat16)
    block_state = jnp.einsum(
        "cjghp,cjgn->cghpn", scaled, b_block, preferred_element_type=jnp.float32
    )
    carry = start_state.astype(jnp.float32)
    begins = []
    for block_index in range(blocks):
        begins.append(carry)
        carry = jnp.exp(cum_end[block_index])[..., None, None] * carry + block_state[block_index]
    begin_half = jnp.stack(begins).astype(jnp.bfloat16)
    carried = jnp.einsum(
        "cign,cghpn->cighp", c_block, begin_half, preferred_element_type=jnp.float32
    )
    summed = (
        inner
        + jnp.exp(cum_block)[..., None] * carried
        + skip_groups[None, None, :, :, None] * x_block
    )
    gate = jax.nn.silu(z_heads.astype(jnp.float32)).reshape(
        blocks, SPAN, group_count, head_count, head_width
    )
    return (summed * gate).reshape(seq_len, group_count, head_count, head_width)


def attend(query, key_pre, value_pre, key_suf, value_suf, prefix_count):
    softmax_scale = 1.0 / math.sqrt(HD)
    score_pre = (
        jnp.einsum("qhd,md->hqm", query, key_pre, preferred_element_type=jnp.float32)
        * softmax_scale
    )
    score_suf = (
        jnp.einsum("qhd,kd->hqk", query, key_suf, preferred_element_type=jnp.float32)
        * softmax_scale
    )
    pre_live = jnp.arange(key_pre.shape[0]) < prefix_count
    causal = jnp.arange(SUF)[:, None] >= jnp.arange(SUF)[None, :]
    score_pre = jnp.where(pre_live[None, None, :], score_pre, NEG_FILL)
    score_suf = jnp.where(causal[None], score_suf, NEG_FILL)
    row_max = jnp.maximum(jnp.max(score_pre, axis=2), jnp.max(score_suf, axis=2))
    weight_pre = jnp.exp(score_pre - row_max[..., None])
    weight_suf = jnp.exp(score_suf - row_max[..., None])
    denominator = jnp.sum(weight_pre, axis=2) + jnp.sum(weight_suf, axis=2)
    mixed = jnp.einsum(
        "hqm,md->qhd",
        weight_pre.astype(jnp.bfloat16),
        value_pre,
        preferred_element_type=jnp.float32,
    )
    mixed = mixed + jnp.einsum(
        "hqk,kd->qhd",
        weight_suf.astype(jnp.bfloat16),
        value_suf,
        preferred_element_type=jnp.float32,
    )
    return mixed / jnp.transpose(denominator)[:, :, None]


def bucket_plan(owner_rows, live_rows, owner_index, capacity):
    positions = jnp.arange(owner_rows.shape[1])
    matches = (
        (owner_rows[:, :, None] == owner_rows[:, None, :])
        & live_rows[:, None, :]
        & (positions[None, None, :] < positions[None, :, None])
    )
    slot_rank = jnp.sum(matches.astype(jnp.int32), axis=2)
    chosen = (
        (owner_rows[:, None, :] == owner_index)
        & live_rows[:, None, :]
        & (slot_rank[:, None, :] == jnp.arange(capacity)[None, :, None])
    )
    return (slot_rank, chosen)


def bucket_send(table, entry_ids, chosen):
    wanted = jnp.sum(jnp.where(chosen, entry_ids[:, None, :], 0), axis=2).reshape(-1)
    filled = jnp.any(chosen, axis=2).reshape(-1)
    picked = jnp.take(table, wanted, axis=0, mode="clip")
    shaped = jnp.where(
        filled.reshape((-1,) + (1,) * (picked.ndim - 1)), picked, jnp.zeros_like(picked)
    )
    return shaped.reshape(chosen.shape[:2] + picked.shape[1:])


def body(
    mixer_input,
    step_raw,
    decay_rate,
    skip_gain,
    state_proj,
    queries,
    suffix_kv,
    state_pool,
    page_pool,
    norm_gain,
    hit_owner,
    hit_slot,
    page_owner,
    page_slot,
    prefix_len,
    suffix_len,
):
    owners = lax.axis_size("owner")
    owner_index = lax.axis_index("owner")
    column = lax.axis_index("tensor")
    local_count = mixer_input.shape[0] // SUF
    local_heads = decay_rate.shape[0]
    local_qheads = queries.shape[1] // HD
    group_index = column * local_heads // (SSM_HEAD_TOTAL // GROUPS)
    kv_index = column * local_qheads // (QHEADS // KVHEADS)
    first_row = owner_index * local_count
    page_capacity = max(2, (local_count * MAXP + owners - 1) // owners * 3 // 2)
    state_owner = hit_owner[:, 0].reshape(owners, local_count)
    state_slot = hit_slot.reshape(owners, local_count)
    every_live = jnp.ones(state_owner.shape, jnp.bool_)
    state_rank, state_pick = bucket_plan(state_owner, every_live, owner_index, CAP_S)
    outgoing = bucket_send(state_pool, state_slot, state_pick)
    arrived = lax.all_to_all(outgoing, "owner", split_axis=0, concat_axis=0, tiled=True)
    arrived = arrived.reshape((owners * CAP_S,) + arrived.shape[2:])
    local_holder = lax.dynamic_index_in_dim(state_owner, owner_index, 0, keepdims=False)
    my_rank = lax.dynamic_index_in_dim(state_rank, owner_index, 0, keepdims=False)
    start_state = jnp.take(arrived, local_holder * CAP_S + my_rank, axis=0, mode="clip")
    x_heads = mixer_input[:, 0].reshape(local_count, SUF, 1, local_heads, MHDIM)
    z_heads = mixer_input[:, 1].reshape(local_count, SUF, 1, local_heads, MHDIM)
    rate_raw = step_raw.reshape(local_count, SUF, 1, local_heads)
    maps_here = lax.dynamic_index_in_dim(state_proj, group_index, 2, keepdims=True)
    b_rows = maps_here[:, 0].reshape(local_count, SUF, 1, STATE)
    c_rows = maps_here[:, 1].reshape(local_count, SUF, 1, STATE)
    core = jax.vmap(mixer_core, in_axes=(0, 0, 0, None, None, 0, 0, 0))
    gated = core(
        x_heads,
        z_heads,
        rate_raw,
        decay_rate.reshape(1, local_heads),
        skip_gain.reshape(1, local_heads),
        b_rows,
        c_rows,
        start_state.reshape(local_count, 1, local_heads, MHDIM, STATE),
    )
    gated = gated.reshape(local_count * SUF, local_heads * MHDIM)
    partial_sum = jnp.sum(gated * gated, axis=1)
    spread = jnp.where(jnp.arange(GROUPS)[:, None] == group_index, partial_sum[None, :], 0.0)
    totals = lax.psum(spread, "tensor")
    square = lax.dynamic_index_in_dim(totals, group_index, 0, keepdims=False) / (
        SSM_HEAD_TOTAL // GROUPS * MHDIM
    )
    my_suffix = lax.dynamic_slice_in_dim(suffix_len, first_row, local_count, 0)
    active = (jnp.arange(SUF)[None, :] < my_suffix[:, None]).reshape(-1)
    rescaled_input = gated * lax.rsqrt(square + EPSILON)[:, None] * norm_gain[None, :]
    mamba_out = jnp.where(active[:, None], rescaled_input, 0.0).astype(jnp.bfloat16)
    pool_head = lax.dynamic_index_in_dim(page_pool, kv_index, 3, keepdims=False)
    entries = local_count * MAXP
    page_rows = page_owner[:, :, 0].reshape(owners, entries)
    page_ids = page_slot.reshape(owners, entries)
    live_rows = (jnp.arange(MAXP)[None, :] * PAGE < prefix_len[:, None]).reshape(owners, entries)
    my_pages = lax.dynamic_index_in_dim(page_rows, owner_index, 0, keepdims=False)
    my_live = lax.dynamic_index_in_dim(live_rows, owner_index, 0, keepdims=False)
    page_rank, page_pick = bucket_plan(page_rows, live_rows, owner_index, page_capacity)
    sending = bucket_send(pool_head, page_ids, page_pick)
    received_rows = lax.all_to_all(sending, "owner", split_axis=0, concat_axis=0, tiled=True)
    received_rows = received_rows.reshape((owners * page_capacity,) + received_rows.shape[2:])
    my_page_rank = lax.dynamic_index_in_dim(page_rank, owner_index, 0, keepdims=False)
    fetched = jnp.take(received_rows, my_pages * page_capacity + my_page_rank, axis=0, mode="clip")
    fetched = jnp.where(my_live[:, None, None, None], fetched, jnp.zeros_like(fetched))
    prefix_kv = fetched.reshape(local_count, MAXP * PAGE, 2, HD)
    my_prefix = lax.dynamic_slice_in_dim(prefix_len, first_row, local_count, 0)
    owned_key_value = lax.dynamic_index_in_dim(suffix_kv, kv_index, 2, keepdims=False).reshape(
        local_count, SUF, 2, HD
    )
    query = queries.reshape(local_count, SUF, local_qheads, HD)
    mixed = jax.vmap(attend)(
        query,
        prefix_kv[:, :, 0],
        prefix_kv[:, :, 1],
        owned_key_value[:, :, 0],
        owned_key_value[:, :, 1],
        my_prefix,
    )
    attn_rows = mixed.reshape(local_count * SUF, local_qheads * HD)
    attn_out = jnp.where(active[:, None], attn_rows, 0.0).astype(jnp.bfloat16)
    return (mamba_out, attn_out)


def solution(mesh):
    return jax.shard_map(
        body,
        mesh=mesh,
        in_specs=(
            P("owner", None, "tensor"),
            P("owner", "tensor"),
            P("tensor"),
            P("tensor"),
            P("owner", None, None, None),
            P("owner", "tensor"),
            P("owner", None, None, None),
            P("owner", "tensor", None, None),
            P("owner", None, None, None, None),
            P("tensor"),
            P(),
            P(),
            P(),
            P(),
            P(),
            P(),
        ),
        out_specs=(P("owner", "tensor"), P("owner", "tensor")),
        check_vma=False,
    )
```

profile of v0, /device:TPU:96, one launch (start us, length us, event | category | flops | bytes accessed | tf_op | source)
XLA Modules:
  0.0 448.7 jit_solution(13598574537655978479)
XLA Ops:
  2.7 4.6 %constant_dynamic-slice_fusion.4 = bf16[16,128,2,1,128]{4,3,2,1,0:T(2,128)(2,1)S(1)} fusion(bf16[16,128,2,4,128]{4,3,2,1,0:T(4,128)(2,1)} %param.24, s32[]{:T(128)S(6)} %select_n.125), kind=kLoop, calls=%fused_computation.95 | loop fusion | bytes 2097156 | tf_op jit(solution)/shard_map/jit(dynamic_index_in_dim)/dynamic_slice | solution.py:193
  9.4 6.0 %gather_fusion.2 = bf16[96,128,2,128]{3,1,2,0:T(8,128)(2,1)} fusion(bf16[16,128,2,128]{3,1,2,0:T(8,128)(2,1)S(1)} %bitcast.137, s32[1024]{0:T(1024)S(1)} %pad_clamp_fusion.1), kind=kCustom, calls=%fused_computation.2 | custom fusion | bytes 12583296 | tf_op jit(solution)/shard_map/jit(_take)/gather | solution.py:120
  15.4 5.9 %broadcast_select_fusion.1 = bf16[16,6,128,2,128]{4,2,3,1,0:T(8,128)(2,1)} fusion(bf16[16,6,128,2,128]{4,2,3,1,0:T(8,128)(2,1)} %bitcast.139, pred[16,6]{1,0:T(8,128)(4,1)S(1)} %copy.187), kind=kLoop, calls=%fused_computation.13 | loop fusion | flops 3145728 | bytes 12583008 | tf_op jit(solution)/shard_map/jit(_where)/select_n | solution.py:121
  21.3 7.8 %all-to-all-start.1 = ((bf16[16,6,128,2,128]{4,2,3,1,0:T(8,128)(2,1)}), bf16[16,6,128,2,128]{4,2,3,1,0:T(8,128)(2,1)}, u32[]{:S(2)}, u32[]{:S(2)}) async-start(bf16[16,6,128,2,128]{4,2,3,1,0:T(8,128)(2,1)} %broadcast_select_fusion.1), calls=%async_computation.1 | async-start | bytes 12582912 | tf_op jit(solution)/shard_map/all_to_all | solution.py:202
  31.2 4.8 %gather_fusion = bf16[32,8,64,256]{3,2,1,0:T(8,128)(2,1)} fusion(bf16[4,8,64,256]{3,2,1,0:T(8,128)(2,1)S(1)} %copy-done.2, s32[1024]{0:T(1024)S(1)} %pad_clamp_fusion.3), kind=kCustom, calls=%fused_computation | custom fusion | bytes 16777344 | tf_op jit(solution)/shard_map/jit(_take)/gather | solution.py:120
  36.0 7.2 %broadcast_select_fusion = bf16[16,2,8,64,256]{4,3,2,1,0:T(8,128)(2,1)} fusion(bf16[16,2,8,64,256]{4,3,2,1,0:T(8,128)(2,1)} %bitcast.138, pred[16,2]{1,0:T(8,128)(4,1)S(1)} %copy.171), kind=kLoop, calls=%fused_computation.12 | loop fusion | flops 4194304 | bytes 16777248 | tf_op jit(solution)/shard_map/jit(_where)/select_n | solution.py:121
  43.2 124.6 %all-to-all-done.1 = bf16[16,6,128,2,128]{4,2,3,1,0:T(8,128)(2,1)} async-done(((bf16[16,6,128,2,128]{4,2,3,1,0:T(8,128)(2,1)}), bf16[16,6,128,2,128]{4,2,3,1,0:T(8,128)(2,1)}, u32[]{:S(2)}, u32[]{:S(2)}) %all-to-all-start.1) | async-done | bytes 6291488 | tf_op jit(solution)/shard_map/all_to_all | solution.py:202
  167.8 5.3 %all-to-all-start = ((bf16[16,2,8,64,256]{4,3,2,1,0:T(8,128)(2,1)}), bf16[16,2,8,64,256]{4,3,2,1,0:T(8,128)(2,1)}, u32[]{:S(2)}, u32[]{:S(2)}) async-start(bf16[16,2,8,64,256]{4,3,2,1,0:T(8,128)(2,1)} %broadcast_select_fusion), calls=%async_computation | async-start | bytes 16777216 | tf_op jit(solution)/shard_map/all_to_all | solution.py:160
  173.1 6.9 %fusion.50 = (bf16[1024,1,512]{2,1,0:T(2,128)(2,1)}, bf16[1024,1,512]{2,1,0:T(2,128)(2,1)}) fusion(bf16[1024,2,512]{2,1,0:T(2,128)(2,1)} %param.16), kind=kLoop, calls=%fused_computation.115 | loop fusion | bytes 4194304 | tf_op jit(solution)/shard_map/slice | solution.py:166
  180.1 5.8 %copy.165 = bf16[1024,1,512]{0,2,1:T(8,128)(2,1)} copy(bf16[1024,1,512]{2,1,0:T(2,128)(2,1)} %get-tuple-element.15) | data formatting | bytes 2097152 | tf_op jit(solution)/shard_map/slice | solution.py:165
  185.9 4.7 %copy_convert_fusion = (f32[1024,1,512]{2,0,1:T(8,128)}, f32[1024,1,512]{2,0,1:T(8,128)}) fusion(bf16[1024,1,512]{2,1,0:T(2,128)(2,1)} %get-tuple-element.14, bf16[1024,1,512]{2,1,0:T(2,128)(2,1)} %get-tuple-element.15), kind=kLoop, calls=%fused_computation.52 | loop fusion | flops 1048576 | bytes 6291456 | tf_op jit(solution)/shard_map/vmap()/convert_element_type | solution.py:62
  190.7 6.1 %copy.182 = f32[1024,1,512]{0,1,2:T(1,128)} copy(f32[1024,1,512]{2,0,1:T(8,128)} %get-tuple-element.26) | data formatting | bytes 4194304 | tf_op jit(solution)/shard_map/vmap()/convert_element_type | solution.py:62
  196.8 6.1 %copy.179 = f32[1024,1,512]{0,1,2:T(1,128)} copy(f32[1024,1,512]{2,0,1:T(8,128)} %get-tuple-element.27) | data formatting | bytes 4194304 | tf_op jit(solution)/shard_map/vmap()/convert_element_type | solution.py:44
  202.9 5.4 %constant_dynamic-slice_fusion.8 = (bf16[1024,1,1,256]{3,2,1,0:T(2,128)(2,1)}, bf16[1024,1,1,256]{3,2,1,0:T(2,128)(2,1)S(1)}) fusion(bf16[1024,2,4,256]{3,2,1,0:T(4,128)(2,1)} %param.20, s32[]{:T(128)S(6)} %select_n.115, s32[]{:T(128)S(6)} %add.163), kind=kLoop, calls=%fused_computation.99 | loop fusion | bytes 2097160 | tf_op jit(solution)/shard_map/slice | solution.py:169
  211.9 2.4 fusion.51
  217.0 2.6 reshape.579
  221.0 2.0 reshape.584
  225.6 2.7 convolution_bitcast_fusion
  229.1 3.3 fusion.6
  232.5 5.9 %gather_fusion.3 = bf16[64,128,2,128]{3,1,2,0:T(8,128)(2,1)} fusion(bf16[96,128,2,128]{3,1,2,0:T(8,128)(2,1)} %bitcast.33, s32[1024]{0:T(1024)S(1)} %pad_clamp_fusion), kind=kCustom, calls=%fused_computation.3 | custom fusion | bytes 8388864 | tf_op jit(solution)/shard_map/jit(_take)/gather | solution.py:205
  238.5 2.5 copy.191
  241.0 2.1 bitcast_select_fusion
  243.1 3.2 bitcast_reduce_fusion
  246.6 4.5 %fusion.1 = f32[4,2,256]{2,1,0:T(2,128)S(1)} fusion(f32[4,2048,256,2]{2,1,3,0:T(8,128)S(1)} %get-tuple-element.23, f32[4,2,256]{2,1,0:T(2,128)S(1)} %max.43, pred[4,2048]{1,0:T(4,128)(4,1)S(1)} %iota_compare_fusion.3), kind=kLoop, calls=%fused_computation.8 | loop fusion | flops 16775168 | bytes 16801792 | tf_op jit(solution)/shard_map/vmap()/reduce_sum | solution.py:85
  251.2 4.7 %fusion.3 = f32[4,128,2,256]{3,1,2,0:T(8,128)S(1)} fusion(f32[4,2048,256,2]{2,1,3,0:T(8,128)S(1)} %get-tuple-element.23, f32[4,2,256]{2,1,0:T(2,128)S(1)} %max.43, pred[4,2048]{1,0:T(4,128)(4,1)S(1)} %iota_compare_fusion.3, bf16[4,2048,2,128]{3,1,0,2:T(8,128)(2,1)S(1)} %bitcast_select_fusion), kind=kOutput, calls=%fused_computation.10 | convolution fusion | flops 1090519040 | bytes 19939328 | tf_op jit(solution)/shard_map/vmap(hqm,md->qhd)/dot_general | solution.py:86
  259.5 97.2 %all-to-all-done = bf16[16,2,8,64,256]{4,3,2,1,0:T(8,128)(2,1)} async-done(((bf16[16,2,8,64,256]{4,3,2,1,0:T(8,128)(2,1)}), bf16[16,2,8,64,256]{4,3,2,1,0:T(8,128)(2,1)}, u32[]{:S(2)}, u32[]{:S(2)}) %all-to-all-start) | async-done | bytes 8388640 | tf_op jit(solution)/shard_map/all_to_all | solution.py:160
  356.8 4.0 gather_fusion.1
  360.8 2.0 fusion.9
  363.6 2.6 multiply_reduce_fusion
  367.8 2.7 reshape.582
  370.7 74.6 %psum.7 = f32[4,1024]{1,0:T(4,128)S(1)} all-reduce(f32[4,1024]{1,0:T(4,128)S(1)} %broadcast_select_fusion.2), channel_id=1, replica_groups=mesh['owner'=16,'tensor'=16] {'tensor'}, use_global_device_ids=true, to_apply=%region_5.6 | all-reduce | flops 4096 | bytes 32768 | tf_op jit(solution)/shard_map/psum | solution.py:185
  445.3 2.0 select_convert_fusion
  (116 shorter events, 25.0 us)
Async XLA Ops:
  0.6 222.6 %copy-start = (bf16[1024,2,4,128]{3,2,1,0:T(4,128)(2,1)S(1)}, bf16[1024,2,4,128]{3,2,1,0:T(4,128)(2,1)}, u32[]{:S(2)}) copy-start(bf16[1024,2,4,128]{3,2,1,0:T(4,128)(2,1)} %param.22) | copy-start | bytes 6291460
  7.3 0.7 copy-start.11
  21.3 7.8 %copy-start.14 = (s32[64]{0:T(128)S(1)}, s32[64]{0:T(128)}, u32[]{:S(2)}) copy-start(s32[64]{0:T(128)} %param.27) | copy-start | bytes 772
  21.3 8.5 %copy-start.16 = (s32[64,1]{0,1:T(1,128)S(1)}, s32[64,1]{0,1:T(1,128)}, u32[]{:S(2)}) copy-start(s32[64,1]{0,1:T(1,128)} %param.26) | copy-start | bytes 772
  21.3 9.9 %copy-start.2 = (bf16[4,8,64,256]{3,2,1,0:T(8,128)(2,1)S(1)}, bf16[4,8,64,256]{3,2,1,0:T(8,128)(2,1)}, u32[]{:S(2)}) copy-start(bf16[4,8,64,256]{3,2,1,0:T(8,128)(2,1)} %param.23) | copy-start | bytes 3145732
  21.3 146.5 %all-to-all-start.1 = ((bf16[16,6,128,2,128]{4,2,3,1,0:T(8,128)(2,1)}), bf16[16,6,128,2,128]{4,2,3,1,0:T(8,128)(2,1)}, u32[]{:S(2)}, u32[]{:S(2)}) async-start(bf16[16,6,128,2,128]{4,2,3,1,0:T(8,128)(2,1)} %broadcast_select_fusion.1), calls=%async_computation.1 | async-start | bytes 12582912 | tf_op jit(solution)/shard_map/all_to_all | solution.py:202
  167.8 189.0 %all-to-all-start = ((bf16[16,2,8,64,256]{4,3,2,1,0:T(8,128)(2,1)}), bf16[16,2,8,64,256]{4,3,2,1,0:T(8,128)(2,1)}, u32[]{:S(2)}, u32[]{:S(2)}) async-start(bf16[16,2,8,64,256]{4,3,2,1,0:T(8,128)(2,1)} %broadcast_select_fusion), calls=%async_computation | async-start | bytes 16777216 | tf_op jit(solution)/shard_map/all_to_all | solution.py:160
  202.9 5.5 %copy-start.10 = (f32[1024,8]{0,1:T(8,128)S(1)}, f32[1024,8]{0,1:T(8,128)}, u32[]{:S(2)}) copy-start(f32[1024,8]{0,1:T(8,128)} %param.17) | copy-start | bytes 98308
  208.2 1.1 copy-start.13
  215.6 5.1 %copy-start.15 = (s32[64]{0:T(128)S(1)}, s32[64]{0:T(128)}, u32[]{:S(2)}) copy-start(s32[64]{0:T(128)} %param.30) | copy-start | bytes 772
  215.6 5.2 %copy-start.17 = (s32[64]{0:T(128)S(1)}, s32[64]{0:T(128)}, u32[]{:S(2)}) copy-start(s32[64]{0:T(128)} %param.31) | copy-start | bytes 772
  223.1 1.6 copy-start.3
  224.4 4.2 copy-start.6
  225.5 3.1 copy-start.8
  241.0 2.1 copy-start.9
  251.2 4.8 %copy-start.7 = (bf16[1024,2,1,128]{3,0,1,2:T(8,128)(2,1)S(1)}, bf16[1024,2,1,128]{3,0,1,2:T(8,128)(2,1)}, u32[]{:S(2)}) copy-start(bf16[1024,2,1,128]{3,0,1,2:T(8,128)(2,1)} %copy-done.6) | copy-start | bytes 1572868
  360.8 2.2 copy-start.4
  360.8 2.8 copy-start.5
  360.8 2.8 copy-start.18
  367.8 77.5 %copy-start.12 = (f32[512]{0:T(512)S(1)}, f32[512]{0:T(512)}, u32[]{:S(2)}) copy-start(f32[512]{0:T(512)} %param.25) | copy-start | bytes 6148
  445.3 3.4 copy-start.1
where the time goes:
time: 450 us; the launch traced here: 449 us
  waiting for transfers between devices  222 us (49%)
  local copies, waits for them, and re-layouts  82.6 us (18%)
  blocking collectives  74.6 us (17%)
  other arithmetic  36.9 us (8%)
  matrix products  18.6 us (4%)
  starting transfers between devices  13.1 us (3%)
    all_to_all x1, waiting for transfers between devices, body(): lax.all_to_all(sending, 'owner', split_axis=0, concat_axis=0, tiled=True)  125 us
    all_to_all x1, waiting for transfers between devices, body(): lax.all_to_all(outgoing, 'owner', split_axis=0, concat_axis=0, tiled=True)  97.2 us
    psum x1, blocking collectives, body(): totals = lax.psum(spread, 'tensor')  74.6 us
    select_n x2, other arithmetic, bucket_send(): jnp.where(filled.reshape((-1,) + (1,) * (picked.ndim - 1)), picked, jnp.z...  13.1 us
    gather x2, local copies, waits for them, and re-layouts, bucket_send(): picked = jnp.take(table, wanted, axis=0, mode='clip')  10.8 us
  transfers between devices with their start and end apart: 2, of which 2 were waited for; matrix products, arithmetic and copies ran while one was open for 22% of the time, Pallas kernels for 0%

commit v1 on v0

--- a/solution.py
+++ b/solution.py
@@ -182,7 +182,9 @@
     gated = gated.reshape(local_count * SUF, local_heads * MHDIM)
     partial_sum = jnp.sum(gated * gated, axis=1)
     spread = jnp.where(jnp.arange(GROUPS)[:, None] == group_index, partial_sum[None, :], 0.0)
-    totals = lax.psum(spread, "tensor")
+    totals = spread
+    for hop in (1, 2, 4, 8):
+        totals = totals + lax.ppermute(totals, "tensor", [(dev, dev ^ hop) for dev in range(16)])
     square = lax.dynamic_index_in_dim(totals, group_index, 0, keepdims=False) / (
         SSM_HEAD_TOTAL // GROUPS * MHDIM
     )

time: 450 us -> 397 us (0.88)
  blocking collectives: 74.6 us -> 0 us
  starting transfers between devices: 13.1 us -> 22.6 us
  waiting for transfers between devices: 222 us -> 229 us
    psum x1 -> x0, blocking collectives: 74.6 us -> none  [body(): totals = lax.psum(spread, 'tensor')]
    ppermute x0 -> x4, starting transfers between devices: none -> 9.49 us  [body(): lax.ppermute(totals, 'tensor', [(dev, dev ^ hop) for dev in range(16)])]
    ppermute x0 -> x4, waiting for transfers between devices: none -> 5.26 us  [body(): lax.ppermute(totals, 'tensor', [(dev, dev ^ hop) for dev in range(16)])]
  transfers between devices with their start and end apart: 2 -> 6, of which waited for: 2 -> 5; matrix products, arithmetic and copies ran while one was open for 22% -> 27% of each run, Pallas kernels for 0% -> 0%
where the time goes in v1:
time: 397 us; the launch traced here: 394 us
  waiting for transfers between devices  229 us (58%)
  local copies, waits for them, and re-layouts  83.3 us (21%)
  other arithmetic  37 us (9%)
  starting transfers between devices  22.6 us (6%)
  matrix products  20.9 us (5%)
    all_to_all x1, waiting for transfers between devices, body(): lax.all_to_all(sending, 'owner', split_axis=0, concat_axis=0, tiled=True)  125 us
    all_to_all x1, waiting for transfers between devices, body(): lax.all_to_all(outgoing, 'owner', split_axis=0, concat_axis=0, tiled=True)  99.2 us
    select_n x2, other arithmetic, bucket_send(): jnp.where(filled.reshape((-1,) + (1,) * (picked.ndim - 1)), picked, jnp.z...  13.1 us
    gather x2, local copies, waits for them, and re-layouts, bucket_send(): picked = jnp.take(table, wanted, axis=0, mode='clip')  10.8 us
    ppermute x4, starting transfers between devices, body(): lax.ppermute(totals, 'tensor', [(dev, dev ^ hop) for dev in range(16)])  9.49 us
    gather x2, local copies, waits for them, and re-layouts, body(): jnp.take(received_rows, my_pages * page_capacity + my_page_rank, axis=0,...  8.44 us
  transfers between devices with their start and end apart: 6, of which 5 were waited for; matrix products, arithmetic and copies ran while one was open for 27% of the time, Pallas kernels for 0%

profile of v1, /device:TPU:96, one launch (start us, length us, event | category | flops | bytes accessed | tf_op | source)
XLA Modules:
  0.0 393.9 jit_solution(2371737875186227969)
XLA Ops:
  2.7 4.6 %constant_dynamic-slice_fusion.4 = bf16[16,128,2,1,128]{4,3,2,1,0:T(2,128)(2,1)S(1)} fusion(bf16[16,128,2,4,128]{4,3,2,1,0:T(4,128)(2,1)} %param.24, s32[]{:T(128)S(6)} %select_n.125), kind=kLoop, calls=%fused_computation.97 | loop fusion | bytes 2097156 | tf_op jit(solution)/shard_map/jit(dynamic_index_in_dim)/dynamic_slice | solution.py:195
  9.4 6.0 %gather_fusion.2 = bf16[96,128,2,128]{3,1,2,0:T(8,128)(2,1)} fusion(bf16[16,128,2,128]{3,1,2,0:T(8,128)(2,1)S(1)} %bitcast.137, s32[1024]{0:T(1024)S(1)} %pad_clamp_fusion.1), kind=kCustom, calls=%fused_computation.2 | custom fusion | bytes 12583296 | tf_op jit(solution)/shard_map/jit(_take)/gather | solution.py:120
  15.4 5.9 %broadcast_select_fusion.1 = bf16[16,6,128,2,128]{4,2,3,1,0:T(8,128)(2,1)} fusion(bf16[16,6,128,2,128]{4,2,3,1,0:T(8,128)(2,1)} %bitcast.139, pred[16,6]{1,0:T(8,128)(4,1)S(1)} %copy.187), kind=kLoop, calls=%fused_computation.13 | loop fusion | flops 3145728 | bytes 12583008 | tf_op jit(solution)/shard_map/jit(_where)/select_n | solution.py:121
  21.3 7.8 %all-to-all-start.1 = ((bf16[16,6,128,2,128]{4,2,3,1,0:T(8,128)(2,1)}), bf16[16,6,128,2,128]{4,2,3,1,0:T(8,128)(2,1)}, u32[]{:S(2)}, u32[]{:S(2)}) async-start(bf16[16,6,128,2,128]{4,2,3,1,0:T(8,128)(2,1)} %broadcast_select_fusion.1), calls=%async_computation.1 | async-start | bytes 12582912 | tf_op jit(solution)/shard_map/all_to_all | solution.py:204
  31.2 4.8 %gather_fusion = bf16[32,8,64,256]{3,2,1,0:T(8,128)(2,1)} fusion(bf16[4,8,64,256]{3,2,1,0:T(8,128)(2,1)S(1)} %copy-done.2, s32[1024]{0:T(1024)S(1)} %pad_clamp_fusion.3), kind=kCustom, calls=%fused_computation | custom fusion | bytes 16777344 | tf_op jit(solution)/shard_map/jit(_take)/gather | solution.py:120
  36.0 7.2 %broadcast_select_fusion = bf16[16,2,8,64,256]{4,3,2,1,0:T(8,128)(2,1)} fusion(bf16[16,2,8,64,256]{4,3,2,1,0:T(8,128)(2,1)} %bitcast.138, pred[16,2]{1,0:T(8,128)(4,1)S(1)} %copy.171), kind=kLoop, calls=%fused_computation.12 | loop fusion | flops 4194304 | bytes 16777248 | tf_op jit(solution)/shard_map/jit(_where)/select_n | solution.py:121
  43.2 124.6 %all-to-all-done.1 = bf16[16,6,128,2,128]{4,2,3,1,0:T(8,128)(2,1)} async-done(((bf16[16,6,128,2,128]{4,2,3,1,0:T(8,128)(2,1)}), bf16[16,6,128,2,128]{4,2,3,1,0:T(8,128)(2,1)}, u32[]{:S(2)}, u32[]{:S(2)}) %all-to-all-start.1) | async-done | bytes 6291488 | tf_op jit(solution)/shard_map/all_to_all | solution.py:204
  167.8 5.3 %all-to-all-start = ((bf16[16,2,8,64,256]{4,3,2,1,0:T(8,128)(2,1)}), bf16[16,2,8,64,256]{4,3,2,1,0:T(8,128)(2,1)}, u32[]{:S(2)}, u32[]{:S(2)}) async-start(bf16[16,2,8,64,256]{4,3,2,1,0:T(8,128)(2,1)} %broadcast_select_fusion), calls=%async_computation | async-start | bytes 16777216 | tf_op jit(solution)/shard_map/all_to_all | solution.py:160
  173.1 6.9 %fusion.52 = (bf16[1024,1,512]{2,1,0:T(2,128)(2,1)}, bf16[1024,1,512]{2,1,0:T(2,128)(2,1)}) fusion(bf16[1024,2,512]{2,1,0:T(2,128)(2,1)} %param.16), kind=kLoop, calls=%fused_computation.118 | loop fusion | bytes 4194304 | tf_op jit(solution)/shard_map/slice | solution.py:166
  180.1 5.8 %copy.165 = bf16[1024,1,512]{0,2,1:T(8,128)(2,1)} copy(bf16[1024,1,512]{2,1,0:T(2,128)(2,1)} %get-tuple-element.15) | data formatting | bytes 2097152 | tf_op jit(solution)/shard_map/slice | solution.py:165
  185.9 4.7 %copy_convert_fusion = (f32[1024,1,512]{2,0,1:T(8,128)}, f32[1024,1,512]{2,0,1:T(8,128)}) fusion(bf16[1024,1,512]{2,1,0:T(2,128)(2,1)} %get-tuple-element.14, bf16[1024,1,512]{2,1,0:T(2,128)(2,1)} %get-tuple-element.15), kind=kLoop, calls=%fused_computation.52 | loop fusion | flops 1048576 | bytes 6291456 | tf_op jit(solution)/shard_map/vmap()/convert_element_type | solution.py:62
  190.7 6.1 %copy.182 = f32[1024,1,512]{0,1,2:T(1,128)} copy(f32[1024,1,512]{2,0,1:T(8,128)} %get-tuple-element.26) | data formatting | bytes 4194304 | tf_op jit(solution)/shard_map/vmap()/convert_element_type | solution.py:62
  196.8 6.1 %copy.179 = f32[1024,1,512]{0,1,2:T(1,128)} copy(f32[1024,1,512]{2,0,1:T(8,128)} %get-tuple-element.27) | data formatting | bytes 4194304 | tf_op jit(solution)/shard_map/vmap()/convert_element_type | solution.py:44
  202.9 5.4 %constant_dynamic-slice_fusion.8 = (bf16[1024,1,1,256]{3,2,1,0:T(2,128)(2,1)}, bf16[1024,1,1,256]{3,2,1,0:T(2,128)(2,1)S(1)}) fusion(bf16[1024,2,4,256]{3,2,1,0:T(4,128)(2,1)} %param.20, s32[]{:T(128)S(6)} %select_n.115, s32[]{:T(128)S(6)} %add.177), kind=kLoop, calls=%fused_computation.101 | loop fusion | bytes 2097160 | tf_op jit(solution)/shard_map/slice | solution.py:169
  211.9 2.4 fusion.53
  217.0 2.6 reshape.579
  225.6 2.7 convolution_bitcast_fusion
  230.5 3.2 fusion.6
  233.8 5.9 %gather_fusion.3 = bf16[64,128,2,128]{3,1,2,0:T(8,128)(2,1)} fusion(bf16[96,128,2,128]{3,1,2,0:T(8,128)(2,1)} %bitcast.33, s32[1024]{0:T(1024)S(1)} %pad_clamp_fusion), kind=kCustom, calls=%fused_computation.3 | custom fusion | bytes 8388864 | tf_op jit(solution)/shard_map/jit(_take)/gather | solution.py:207
  239.7 2.5 copy.191
  242.3 2.1 bitcast_select_fusion
  244.4 3.2 bitcast_reduce_fusion
  247.6 4.5 %fusion.1 = f32[4,2,256]{2,1,0:T(2,128)S(1)} fusion(f32[4,2048,256,2]{2,1,3,0:T(8,128)S(1)} %get-tuple-element.23, f32[4,2,256]{2,1,0:T(2,128)S(1)} %max.43, pred[4,2048]{1,0:T(4,128)(4,1)S(1)} %iota_compare_fusion.3), kind=kLoop, calls=%fused_computation.8 | loop fusion | flops 16775168 | bytes 16801792 | tf_op jit(solution)/shard_map/vmap()/reduce_sum | solution.py:85
  252.1 5.5 %fusion.3 = f32[4,128,2,256]{3,1,2,0:T(8,128)} fusion(f32[4,2048,256,2]{2,1,3,0:T(8,128)S(1)} %get-tuple-element.23, f32[4,2,256]{2,1,0:T(2,128)S(1)} %max.43, pred[4,2048]{1,0:T(4,128)(4,1)S(1)} %iota_compare_fusion.3, bf16[4,2048,2,128]{3,1,0,2:T(8,128)(2,1)S(1)} %bitcast_select_fusion), kind=kOutput, calls=%fused_computation.10 | convolution fusion | flops 1090519040 | bytes 19939328 | tf_op jit(solution)/shard_map/vmap(hqm,md->qhd)/dot_general | solution.py:86
  257.6 99.2 %all-to-all-done = bf16[16,2,8,64,256]{4,3,2,1,0:T(8,128)(2,1)} async-done(((bf16[16,2,8,64,256]{4,3,2,1,0:T(8,128)(2,1)}), bf16[16,2,8,64,256]{4,3,2,1,0:T(8,128)(2,1)}, u32[]{:S(2)}, u32[]{:S(2)}) %all-to-all-start) | async-done | bytes 8388640 | tf_op jit(solution)/shard_map/all_to_all | solution.py:160
  356.8 4.0 %gather_fusion.1 = bf16[4,8,64,256]{3,2,1,0:T(8,128)(2,1)S(1)} fusion(bf16[32,8,64,256]{3,2,1,0:T(8,128)(2,1)} %bitcast.13, s32[1024]{0:T(1024)S(1)} %pad_clamp_fusion.2), kind=kCustom, calls=%fused_computation.1 | custom fusion | bytes 2097168 | tf_op jit(solution)/shard_map/jit(_take)/gather | solution.py:164
  363.6 3.7 multiply_reduce_fusion
  371.2 3.2 collective-permute-start.1
  374.4 2.0 collective-permute-done.1
  380.3 3.2 collective-permute-start.3
  384.5 3.2 copy.185
  387.7 2.7 reshape.582
  (130 shorter events, 35.5 us)
Async XLA Ops:
  0.6 222.6 %copy-start = (bf16[1024,2,4,128]{3,2,1,0:T(4,128)(2,1)S(1)}, bf16[1024,2,4,128]{3,2,1,0:T(4,128)(2,1)}, u32[]{:S(2)}) copy-start(bf16[1024,2,4,128]{3,2,1,0:T(4,128)(2,1)} %param.22) | copy-start | bytes 6291460
  7.3 0.7 copy-start.12
  21.3 7.8 %copy-start.15 = (s32[64]{0:T(128)S(1)}, s32[64]{0:T(128)}, u32[]{:S(2)}) copy-start(s32[64]{0:T(128)} %param.27) | copy-start | bytes 772
  21.3 8.5 %copy-start.17 = (s32[64,1]{0,1:T(1,128)S(1)}, s32[64,1]{0,1:T(1,128)}, u32[]{:S(2)}) copy-start(s32[64,1]{0,1:T(1,128)} %param.26) | copy-start | bytes 772
  21.3 9.9 %copy-start.2 = (bf16[4,8,64,256]{3,2,1,0:T(8,128)(2,1)S(1)}, bf16[4,8,64,256]{3,2,1,0:T(8,128)(2,1)}, u32[]{:S(2)}) copy-start(bf16[4,8,64,256]{3,2,1,0:T(8,128)(2,1)} %param.23) | copy-start | bytes 3145732
  21.3 146.5 %all-to-all-start.1 = ((bf16[16,6,128,2,128]{4,2,3,1,0:T(8,128)(2,1)}), bf16[16,6,128,2,128]{4,2,3,1,0:T(8,128)(2,1)}, u32[]{:S(2)}, u32[]{:S(2)}) async-start(bf16[16,6,128,2,128]{4,2,3,1,0:T(8,128)(2,1)} %broadcast_select_fusion.1), calls=%async_computation.1 | async-start | bytes 12582912 | tf_op jit(solution)/shard_map/all_to_all | solution.py:204
  167.8 189.0 %all-to-all-start = ((bf16[16,2,8,64,256]{4,3,2,1,0:T(8,128)(2,1)}), bf16[16,2,8,64,256]{4,3,2,1,0:T(8,128)(2,1)}, u32[]{:S(2)}, u32[]{:S(2)}) async-start(bf16[16,2,8,64,256]{4,3,2,1,0:T(8,128)(2,1)} %broadcast_select_fusion), calls=%async_computation | async-start | bytes 16777216 | tf_op jit(solution)/shard_map/all_to_all | solution.py:160
  202.9 5.5 %copy-start.11 = (f32[1024,8]{0,1:T(8,128)S(1)}, f32[1024,8]{0,1:T(8,128)}, u32[]{:S(2)}) copy-start(f32[1024,8]{0,1:T(8,128)} %param.17) | copy-start | bytes 98308
  208.2 1.1 copy-start.14
  215.6 5.1 %copy-start.16 = (s32[64]{0:T(128)S(1)}, s32[64]{0:T(128)}, u32[]{:S(2)}) copy-start(s32[64]{0:T(128)} %param.30) | copy-start | bytes 772
  215.6 5.2 %copy-start.18 = (s32[64]{0:T(128)S(1)}, s32[64]{0:T(128)}, u32[]{:S(2)}) copy-start(s32[64]{0:T(128)} %param.31) | copy-start | bytes 772
  223.1 1.6 copy-start.3
  224.4 4.2 %copy-start.7 = (bf16[1024,2,1,128]{3,0,1,2:T(8,128)(2,1)}, bf16[1024,2,1,128]{3,0,1,2:T(8,128)(2,1)S(1)}, u32[]{:S(2)}) copy-start(bf16[1024,2,1,128]{3,0,1,2:T(8,128)(2,1)S(1)} %copy.193) | copy-start | bytes 1572868
  225.5 3.1 copy-start.9
  242.2 2.1 copy-start.10
  360.8 2.2 copy-start.4
  360.8 2.8 copy-start.5
  360.8 2.8 copy-start.19
  363.6 5.4 %copy-start.6 = (f32[4,2,256,256]{2,3,1,0:T(8,128)S(1)}, f32[4,2,256,256]{2,3,1,0:T(8,128)}, u32[]{:S(2)}) copy-start(f32[4,2,256,256]{2,3,1,0:T(8,128)} %get-tuple-element.25) | copy-start | bytes 6291460
  367.3 10.8 %copy-start.8 = (bf16[1024,2,1,128]{3,0,1,2:T(8,128)(2,1)S(1)}, bf16[1024,2,1,128]{3,0,1,2:T(8,128)(2,1)}, u32[]{:S(2)}) copy-start(bf16[1024,2,1,128]{3,0,1,2:T(8,128)(2,1)} %copy-done.7) | copy-start | bytes 1572868
  367.3 10.8 %copy-start.20 = (f32[4,128,2,256]{3,1,2,0:T(8,128)S(1)}, f32[4,128,2,256]{3,1,2,0:T(8,128)}, u32[]{:S(2)}) copy-start(f32[4,128,2,256]{3,1,2,0:T(8,128)} %fusion.3) | copy-start | bytes 3145732
  367.4 3.8 collective-permute-start
  371.2 5.3 %collective-permute-start.1 = (f32[4,1024]{1,0:T(4,128)S(1)}, f32[4,1024]{1,0:T(4,128)S(1)}, u32[]{:S(2)}, u32[]{:S(2)}) collective-permute-start(f32[4,1024]{1,0:T(4,128)S(1)} %fusion.48), channel_id=1, source_target_pairs={{0,2},{1,3},{2,0},{3,1},{4,6},{5,7},{6,4},{7,5},{8,10},{9,11},{10,... | collective-permute-start | bytes 49160 | tf_op jit(solution)/shard_map/ppermute | solution.py:187
  376.6 3.8 collective-permute-start.2
  380.3 10.1 %collective-permute-start.3 = (f32[4,1024]{1,0:T(4,128)S(1)}, f32[4,1024]{1,0:T(4,128)S(1)}, u32[]{:S(2)}, u32[]{:S(2)}) collective-permute-start(f32[4,1024]{1,0:T(4,128)S(1)} %add.161), channel_id=1, source_target_pairs={{0,8},{1,9},{2,10},{3,11},{4,12},{5,13},{6,14},{7,15},{8,0},{9,1},... | collective-permute-start | bytes 49160 | tf_op jit(solution)/shard_map/ppermute | solution.py:187
  387.7 2.8 copy-start.13
  390.5 3.4 copy-start.1
